TPU v7x, 128 devices: a whole 4x4x4 slice. The times are simulated.
128 devices in a mesh: head: 8 (over z, core), ctx: 16 (over x, y).
Axes of the slice: x: 4, y: 4, z: 4, core: 2. Of those that a mesh axis runs over, the one named last changes fastest.
Arguments:
- queries: bfloat16 [16384, 8, 128], P('ctx', 'head'), may hold values from -120 to 120
- keys: bfloat16 [16384, 8, 128], P('ctx', 'head'), may hold values from -6 to 6
- values: bfloat16 [16384, 8, 128], P('ctx', 'head'), may hold values from -6 to 6
- house: bfloat16 [16384, 8, 128], P('ctx', 'head'), may hold values from -6 to 6
- rates: float32 [8, 16384], P('head', 'ctx'), may hold values from 0.0002 to 1.9, as said below
- out_weight: bfloat16 [1024, 8192], P('head'), may hold values from -0.25 to 0.25
Outputs:
- attended: bfloat16 [16384, 8, 128], P('ctx', 'head')
- projected: bfloat16 [16384, 8192], P('ctx', 'head')
Inputs may be any that keep to these rules, and one draw needn't show every extreme that they name: `rates`: strictly positive and below 2, so every transition is a contraction.
All inputs are finite; a program needn't handle non-finite values.
Results may differ from a plain program's by a relative error of at most 0.015.
Values may be sent and summed in bfloat16 or wider, within the bound.
No kernel may reach another device: no remote copies, remote signals or barrier semaphores. Data moves between devices by JAX's collectives and lax.ppermute only.
A program may use at most 64 MiB of HBM per device.

v0:
```python
import jax
import jax.numpy as jnp
from jax import lax
from jax.sharding import PartitionSpec as P

BLOCK = 128


EPSILON = 1e-06
NEGATIVE = -1e30
PRECISE = lax.Precision.HIGHEST


def from_everyone(x, axis):
    count = lax.axis_size(axis)
    return lax.all_to_all(jnp.broadcast_to(x[None], (count, *x.shape)), axis, 0, 0, tiled=True)


def joined_along(blocks, dim):
    blocks = jnp.moveaxis(blocks, 0, dim)
    shape = blocks.shape
    return blocks.reshape(*shape[:dim], shape[dim] * shape[dim + 1], *shape[dim + 2 :])


def collect(x, axis, dim):
    blocks = from_everyone(x, axis)
    return joined_along(blocks, dim)


def matmul(first_matrix, second_matrix):
    return jnp.matmul(first_matrix, second_matrix, precision=PRECISE)


def block_parts(query_rows, key_rows, house_rows, decays):
    length = query_rows.shape[0]
    features = query_rows.shape[1]
    row_index = lax.broadcasted_iota(jnp.int32, (length, length), 0)
    col_index = lax.broadcasted_iota(jnp.int32, (length, length), 1)
    gram_matrix = matmul(house_rows, house_rows.T)
    zero_block = jnp.zeros_like(gram_matrix)
    lower_part = jnp.where(row_index > col_index, gram_matrix, zero_block) + jnp.diag(1.0 / decays)
    identity = jnp.eye(length, dtype=query_rows.dtype)
    inverse = jax.scipy.linalg.solve_triangular(lower_part, identity, lower=True)
    left_part = jnp.where(row_index >= col_index, matmul(query_rows, house_rows.T), zero_block)
    right_part = matmul(
        inverse, jnp.where(row_index > col_index, matmul(house_rows, key_rows.T), zero_block)
    )
    start_query = query_rows - matmul(matmul(left_part, inverse), house_rows)
    final_key = key_rows - matmul(right_part.T, house_rows)
    inside_mask = matmul(query_rows, key_rows.T) - matmul(left_part, right_part)
    inside_mask = jnp.where(row_index >= col_index, inside_mask, NEGATIVE)
    passage = jnp.eye(features, dtype=query_rows.dtype) - matmul(
        house_rows.T, matmul(inverse, house_rows)
    )
    return (start_query, final_key, inside_mask, passage)


def shard_local(start_query, final_key, inside_mask, passage):
    blocks, length, features = start_query.shape
    rows_dev = blocks * length
    col_block = lax.broadcasted_iota(jnp.int32, (length, rows_dev), 1) // length
    anchor = jnp.zeros((), jnp.int32)

    def advance(running, element):
        moved_keys, prefix = running
        number, query_rows, key_rows, inside_rows, passage_rows = element
        across = matmul(query_rows, moved_keys.T)
        scores = jnp.where(col_block < number, across, NEGATIVE)
        scores = lax.dynamic_update_slice(scores, inside_rows, (anchor, number * length))
        carried_query = matmul(query_rows, prefix)
        moved_keys = matmul(moved_keys, passage_rows.T)
        moved_keys = lax.dynamic_update_slice(moved_keys, key_rows, (number * length, anchor))
        prefix = matmul(passage_rows, prefix)
        return ((moved_keys, prefix), (scores, carried_query))

    numbers = jnp.arange(blocks, dtype=jnp.int32)
    initial = (
        jnp.zeros((rows_dev, features), start_query.dtype),
        jnp.eye(features, dtype=start_query.dtype),
    )
    (end_keys, transit), (scores, carried) = lax.scan(
        advance, initial, (numbers, start_query, final_key, inside_mask, passage)
    )
    return (
        scores.reshape(rows_dev, rows_dev),
        carried.reshape(rows_dev, features),
        end_keys,
        transit,
    )


def transfer_table(all_ends, number):
    features = all_ends.shape[1]

    def gradient_pass(running, element):
        source, passage = element
        before = source < number
        projected_result = jnp.where(before, running, jnp.zeros_like(running))
        running = jnp.where(before, matmul(running, passage), running)
        return (running, projected_result)

    sources = jnp.arange(all_ends.shape[0], dtype=jnp.int32)
    _, transfers = lax.scan(
        gradient_pass, jnp.eye(features, dtype=all_ends.dtype), (sources, all_ends), reverse=True
    )
    return transfers


def absorb(softmax_state, query_start, transfers, key_block, value_block, source, number):
    row_peak, row_total, summed = softmax_state
    clipped = jnp.clip(source, 0, transfers.shape[0] - 1)
    passage = lax.dynamic_index_in_dim(transfers, clipped, 0, keepdims=False)
    moved_query = matmul(query_start, passage)
    scores = matmul(moved_query, key_block.astype(jnp.float32).T)
    usable = jnp.logical_and(source >= 0, source < number)
    scores = jnp.where(usable, scores, NEGATIVE)
    new_peak = jnp.maximum(row_peak, jnp.max(scores, axis=1))
    weight_matrix = jnp.where(usable, jnp.exp(scores - new_peak[:, None]), 0.0)
    shrink = jnp.exp(row_peak - new_peak)
    row_total = row_total * shrink + jnp.sum(weight_matrix, axis=1)
    summed = summed * shrink[:, None] + jnp.dot(
        weight_matrix.astype(jnp.bfloat16), value_block, preferred_element_type=jnp.float32
    )
    return (new_peak, row_total, summed)


def body(queries, keys, values, house, rates, out_weight):
    rows_dev = queries.shape[0]
    features = queries.shape[2]
    number = lax.axis_index("ctx")
    blocks = rows_dev // BLOCK
    query_rows = queries[:, 0, :].astype(jnp.float32) * features ** (-0.5)
    key_rows = keys[:, 0, :].astype(jnp.float32)
    value_rows = values[:, 0, :]
    house_raw = house[:, 0, :].astype(jnp.float32)
    house_unit = house_raw / jnp.sqrt(
        jnp.sum(house_raw * house_raw, axis=1, keepdims=True) + EPSILON
    )
    block_data = jax.vmap(block_parts)(
        query_rows.reshape(blocks, BLOCK, features),
        key_rows.reshape(blocks, BLOCK, features),
        house_unit.reshape(blocks, BLOCK, features),
        rates[0].reshape(blocks, BLOCK),
    )
    local_scores, query_start, end_keys, transit = shard_local(*block_data)
    row_peak = jnp.max(local_scores, axis=1)
    weight_matrix = jnp.exp(local_scores - row_peak[:, None])
    row_total = jnp.sum(weight_matrix, axis=1)
    summed = jnp.dot(
        weight_matrix.astype(jnp.bfloat16), value_rows, preferred_element_type=jnp.float32
    )
    softmax_state = (row_peak, row_total, summed)
    all_ends = collect(transit[None], "ctx", 0)
    transfers = transfer_table(all_ends, number)
    stored_keys = end_keys.astype(jnp.bfloat16)
    running = softmax_state
    key_piece = lax.all_gather(stored_keys, "ctx", axis=0, tiled=True)
    value_piece = lax.all_gather(value_rows, "ctx", axis=0, tiled=True)
    piece_rows = key_piece.shape[0]
    groups = piece_rows // rows_dev
    sources = jnp.arange(groups, dtype=jnp.int32)

    def through(inner_state, element):
        return (
            absorb(inner_state, query_start, transfers, element[0], element[1], element[2], number),
            None,
        )

    running, _ = lax.scan(
        through,
        running,
        (
            key_piece.reshape(groups, rows_dev, features),
            value_piece.reshape(groups, rows_dev, features),
            sources,
        ),
    )
    softmax_state = running
    row_peak, row_total, summed = softmax_state
    attended = (summed / row_total[:, None]).astype(jnp.bfloat16)
    columns = lax.all_to_all(out_weight, "head", split_axis=1, concat_axis=0, tiled=True)
    piece = collect(attended[:, None, :], "head", 1)
    heads_here = piece.shape[1]
    flattened = piece.reshape(piece.shape[0], heads_here * features)
    projected = jnp.dot(flattened, columns, preferred_element_type=jnp.float32)
    return (attended[:, None, :], projected.astype(jnp.bfloat16))


def solution(mesh):
    in_specs = (
        P("ctx", "head", None),
        P("ctx", "head", None),
        P("ctx", "head", None),
        P("ctx", "head", None),
        P("head", "ctx"),
        P("head", None),
    )
    out_specs = (P("ctx", "head", None), P("ctx", "head"))
    return jax.shard_map(body, mesh=mesh, in_specs=in_specs, out_specs=out_specs, check_vma=False)
```

profile of v0, /device:TPU:30, one launch (start us, length us, event | category | flops | bytes accessed | tf_op | source)
XLA Modules:
  0.0 463.4 jit_solution(4570962235549815845)
XLA Ops:
  17.0 79.4 %custom-call.4 = f32[8,1,128,128]{2,3,1,0:T(8,128)S(1)} custom-call(f32[8,1,128,128]{3,2,1,0:T(8,128)} %fusion.46), custom_call_target="InvertDiagBlocksLowerTriangular" | custom-call | tf_op jit(solution)/shard_map/vmap(jit(_solve_triangular))/triangular_solve | solution.py:43
  100.5 3.0 convolution_subtract_fusion.2
  106.2 41.4 %while.52 = (s32[]{:T(128)}, f32[1024,128]{0,1:T(8,128)S(1)}, f32[128,128]{1,0:T(8,128)S(1)}, f32[8,128,1024]{2,1,0:T(8,128)}, f32[8,128,128]{2,1,0:T(8,128)S(1)...) while((s32[]{:T(128)}, f32[1024,128]{0,1:T(8,128)S(1)}, ...), condition=%wide.region_2.3_spmd.clone.clone, body=%wide.region_1.2_spmd.clone.sunk.clone | while | flops 453378048 | bytes 5384915 | solution.py:81
  149.5 7.1 %all-to-all-start = ((f32[16,1,128,128]{3,2,1,0:T(8,128)}), f32[16,1,128,128]{3,2,1,0:T(8,128)S(1)}, u32[]{:S(2)}, u32[]{:S(2)}) async-start(f32[16,1,128,128]{3,2,1,0:T(8,128)} %broadcast_in_dim.121), calls=%async_computation | async-start | bytes 2097152 | tf_op jit(solution)/shard_map/all_to_all | solution.py:16
  157.4 4.3 copy.42
  164.2 3.1 fusion.42
  168.0 3.8 all-to-all-done
  172.9 5.8 %all-to-all-start.2 = ((bf16[128,8,1024]{0,2,1:T(8,128)(2,1)}), bf16[128,8,1024]{0,2,1:T(8,128)(2,1)S(1)}, u32[]{:S(2)}, u32[]{:S(2)}) async-start(bf16[128,8,1024]{0,2,1:T(8,128)(2,1)} %bitcast.27), calls=%async_computation.2 | async-start | bytes 4194304 | tf_op jit(solution)/shard_map/all_to_all | solution.py:181
  179.9 47.1 %while.50 = (s32[]{:T(128)}, f32[128,128]{0,1:T(8,128)S(1)}, f32[16,128,128]{1,2,0:T(8,128)}, s32[16]{0:T(128)S(1)}, s32[]{:T(128)}, /*index=5*/f32[16,128,128]{2,1,0:T(8,128)}) while((s32[]{:T(128)}, f32[128,128]{0,1:T(8,128)S(1)}, f32[16,128,128]{1,2,0:T(8,128)}, s32[16]{0:T(128)S(1)}, s32[]{:T(128)}, ...), condition=%wide.region_6.7_spmd.clone, body=%wide.region_5.6_spmd.sunk.clone | while | flops 25198596 | bytes 524400 | solution.py:103
  227.1 6.4 %copy.47 = bf16[16384,128]{1,0:T(8,128)(2,1)} copy(bf16[16384,128]{0,1:T(8,128)(2,1)} %all-gather.4.cloned.1.call-done) | data formatting | bytes 8388608 | tf_op jit(solution)/shard_map/while | solution.py:169
  233.5 25.0 %all-gather.6.cloned.1.call-done = bf16[16384,1,128]{2,0,1:T(8,128)(2,1)} async-done(((bf16[1024,1,128]{2,0,1:T(8,128)(2,1)}), bf16[16384,1,128]{2,0,1:T(8,128)(2,1)}) %all-gather.6.cloned.1.call-update) | async-done | bytes 4194320 | tf_op jit(solution)/shard_map/all_gather | solution.py:158
  258.5 158.5 %while.51 = (s32[]{:T(128)}, f32[1024]{0:T(1024)S(1)}, f32[1024]{0:T(1024)S(1)}, f32[1024,128]{1,0:T(8,128)S(1)}, s32[16]{0:T(128)S(1)}, /*index=5*/s32[]{:T(128...) while((s32[]{:T(128)}, f32[1024]{0:T(1024)S(1)}, ...), condition=%wide.region_10.11_spmd.clone, body=%wide.region_7.10_spmd.sunk.clone | while | flops 2091124736 | bytes 15860901 | solution.py:169
  262.4 3.0 select_reduce_fusion.3
  282.2 3.0 select_reduce_fusion.3
  292.2 3.0 select_reduce_fusion.3
  321.9 3.0 select_reduce_fusion.3
  331.8 3.0 select_reduce_fusion.3
  361.5 3.0 select_reduce_fusion.3
  371.4 3.0 select_reduce_fusion.3
  401.1 3.0 select_reduce_fusion.3
  411.0 3.0 select_reduce_fusion.3
  418.9 4.4 all-to-all-start.1
  426.9 23.8 %all-to-all-done.1 = bf16[8,1024,1,128]{1,3,2,0:T(8,128)(2,1)} async-done(((bf16[8,1024,1,128]{1,3,2,0:T(8,128)(2,1)}), bf16[8,1024,1,128]{1,3,2,0:T(8,128)(2,1)}, u32[]{:S(2)}, u32[]{:S(2)}) %all-to-all-start.1) | async-done | bytes 2097184 | tf_op jit(solution)/shard_map/all_to_all | solution.py:16
  450.7 5.9 %convolution_convert_fusion = bf16[1024,1024]{1,0:T(8,128)(2,1)} fusion(bf16[1024,1024]{0,1:T(8,128)(2,1)} %bitcast.26, bf16[1024,1024]{1,0:T(8,128)(2,1)} %bitcast.176), kind=kOutput, calls=%fused_computation.55 | convolution fusion | flops 2148532224 | bytes 6291456 | tf_op jit(solution)/shard_map/dot_general | solution.py:185
  (323 shorter events, 203.5 us)
Async XLA Ops:
  7.2 6.4 %copy-start.2 = (bf16[1024,1,128]{2,0,1:T(8,128)(2,1)S(1)}, bf16[1024,1,128]{2,0,1:T(8,128)(2,1)}, u32[]{:S(2)}) copy-start(bf16[1024,1,128]{2,0,1:T(8,128)(2,1)} %param.15) | copy-start | bytes 786436
  7.2 219.9 %all-gather.4.cloned.1.call-start = ((), (), s32[]{:S(2)}) async-start(), calls=%async_computation.3 | async-start | bytes 4456448 | tf_op jit(solution)/shard_map/all_gather | solution.py:157
  99.2 5.0 %copy-start.3 = (bf16[1024,1,128]{2,0,1:T(8,128)(2,1)S(1)}, bf16[1024,1,128]{2,0,1:T(8,128)(2,1)}, u32[]{:S(2)}) copy-start(bf16[1024,1,128]{2,0,1:T(8,128)(2,1)} %param.15) | copy-start | bytes 786436
  149.5 22.3 %all-to-all-start = ((f32[16,1,128,128]{3,2,1,0:T(8,128)}), f32[16,1,128,128]{3,2,1,0:T(8,128)S(1)}, u32[]{:S(2)}, u32[]{:S(2)}) async-start(f32[16,1,128,128]{3,2,1,0:T(8,128)} %broadcast_in_dim.121), calls=%async_computation | async-start | bytes 2097152 | tf_op jit(solution)/shard_map/all_to_all | solution.py:16
  156.6 101.9 %all-gather.6.cloned.1.call-start = ((), (), s32[]{:S(2)}) async-start(), calls=%async_computation.4 | async-start | bytes 4456448 | tf_op jit(solution)/shard_map/all_gather | solution.py:158
  164.2 3.1 copy-start.1
  171.8 1.1 copy-start
  172.9 244.5 %all-to-all-start.2 = ((bf16[128,8,1024]{0,2,1:T(8,128)(2,1)}), bf16[128,8,1024]{0,2,1:T(8,128)(2,1)S(1)}, u32[]{:S(2)}, u32[]{:S(2)}) async-start(bf16[128,8,1024]{0,2,1:T(8,128)(2,1)} %bitcast.27), calls=%async_computation.2 | async-start | bytes 4194304 | tf_op jit(solution)/shard_map/all_to_all | solution.py:181
  418.9 31.7 %all-to-all-start.1 = ((bf16[8,1024,1,128]{1,3,2,0:T(8,128)(2,1)}), bf16[8,1024,1,128]{1,3,2,0:T(8,128)(2,1)}, u32[]{:S(2)}, u32[]{:S(2)}) async-start(bf16[8,1024,1,128]{1,3,2,0:T(8,128)(2,1)} %broadcast_in_dim.123), calls=%async_computation.1 | async-start | bytes 4194304 | tf_op jit(solution)/shard_map/all_to_all | solution.py:16
Sparse Core Ops, SparseCore 0:
  148.5 56.6 all-gather.3
  207.3 51.1 all-gather.5
where the time goes:
time: 471 us; the launch traced here: 463 us
  matrix products  161 us (34%)
  other arithmetic  114 us (24%)
  local copies, waits for them, and re-layouts  56.7 us (12%)
  waiting for transfers between devices  53.4 us (11%)
  loops' own time  46.8 us (10%)
  starting transfers between devices  17.4 us (4%)
  between operations  14.3 us (3%)
    dot_general x91, matrix products, matmul(): return jnp.matmul(first_matrix, second_matrix, precision=PRECISE)  121 us
    another operation x1, other arithmetic, block_parts(): jax.scipy.linalg.solve_triangular(lower_part, identity, lower=True)  79.4 us
    dot_general x16, matrix products, absorb(): jnp.dot(weight_matrix.astype(jnp.bfloat16), value_block, preferred_elemen...  32.8 us
    another operation x1, loops' own time, body(): lax.scan(through, running, (key_piece.reshape(groups, rows_dev, features)...  32.1 us
    all_to_all x2, waiting for transfers between devices, from_everyone(): lax.all_to_all(jnp.broadcast_to(x[None], (count, *x.shape)), axis, 0, 0,...  27.6 us
    all_gather x1, waiting for transfers between devices, body(): value_piece = lax.all_gather(value_rows, 'ctx', axis=0, tiled=True)  25 us
    dynamic_slice x32, local copies, waits for them, and re-layouts, transfer_table(): lax.scan(gradient_pass, jnp.eye(features, dtype=all_ends.dtype), (sources...  18.6 us
    reduce_sum x16, other arithmetic, absorb(): row_total = row_total * shrink + jnp.sum(weight_matrix, axis=1)  13.6 us
  transfers between devices with their start and end apart: 5, of which 3 were waited for; matrix products, arithmetic and copies ran while one was open for 40% of the time, Pallas kernels for 0%

commit v1 on v0

v1 whole, which is shorter than its diff:
```python
import jax
import jax.numpy as jnp
from jax import lax
from jax.experimental import pallas as pl
from jax.experimental.pallas import tpu as pltpu
from jax.sharding import PartitionSpec as P

C = 128
F32 = jnp.float32
BF16 = jnp.bfloat16
EPSILON = 1e-06
NEGATIVE = -1e30
LOG2E = 1.4426950408889634
VMEM_LIMIT = 56 * 1024 * 1024


def split(x):
    high = x.astype(BF16)
    return high, (x - high.astype(F32)).astype(BF16)


def left(x):
    return jnp.concatenate(split(x), axis=1)


def right_nn(x):
    pair = jnp.concatenate(split(x), axis=1)
    return jnp.concatenate([pair, pair], axis=0)


def right_nt(x):
    high, low = split(x)
    return jnp.concatenate(
        [jnp.concatenate([high, high], axis=1), jnp.concatenate([low, low], axis=1)], axis=0
    )


def halves(x):
    return x[:, : x.shape[1] // 2] + x[:, x.shape[1] // 2 :]


def nn(a, b):
    return halves(jnp.dot(a, b, preferred_element_type=F32))


def contract_last(a, b):
    return lax.dot_general(a, b, (((1,), (1,)), ((), ())), preferred_element_type=F32)


def nt(a, b):
    return halves(contract_last(a, b))


def unit_house(house):
    raw = house.astype(F32)
    return raw / jnp.sqrt(jnp.sum(raw * raw, axis=1, keepdims=True) + EPSILON)


def transport_kernel(keys, house, rates, sent, passages, inverses, rights, finals, unit):
    blocks = rates.shape[0]
    row = lax.broadcasted_iota(jnp.int32, (C, C), 0)
    col = lax.broadcasted_iota(jnp.int32, (C, C), 1)
    eye = jnp.where(row == col, 1.0, 0.0).astype(F32)
    every = range(blocks)
    w = [unit_house(house[pl.ds(n * C, C), :]) for n in every]
    for n in every:
        unit[pl.ds(n * C, C), :] = w[n]
    wl = [left(x) for x in w]
    strict = []
    for n in every:
        gram = nt(wl[n], right_nt(w[n]))
        decay = jnp.transpose(jnp.broadcast_to(rates[n : n + 1, :], (C, C)))
        strict.append(jnp.where(row > col, gram, 0.0) * decay)
    x = [eye - jnp.where((row // 2) == (col // 2), strict[n], 0.0) for n in every]
    size = 2
    while size < C:
        band = ((row // (2 * size)) == (col // (2 * size))) & ((row // size) != (col // size))
        inner = [nn(left(jnp.where(band, strict[n], 0.0)), right_nn(x[n])) for n in every]
        x = [x[n] - nn(left(x[n]), right_nn(inner[n])) for n in every]
        size *= 2
    t = [x[n] * rates[n : n + 1, :] for n in every]
    for n in every:
        inverses[n] = t[n]
    final = []
    for n in every:
        k = keys[pl.ds(n * C, C), :]
        met = jnp.where(col > row, contract_last(jnp.concatenate([k, k], axis=1), wl[n]), 0.0)
        r = nt(left(met), right_nt(t[n]))
        rights[n] = r
        f = k.astype(F32) - nn(left(r), right_nn(w[n]))
        finals[pl.ds(n * C, C), :] = f
        final.append(f)
    passage = []
    for n in every:
        u = nn(left(t[n]), right_nn(w[n]))
        passage.append(eye - nn(left(jnp.transpose(w[n])), right_nn(u)))
        passages[n] = passage[n]
    sent[pl.ds((blocks - 1) * C, C), :] = final[blocks - 1].astype(BF16)
    s = passage[blocks - 1]
    for n in range(blocks - 2, -1, -1):
        sent[pl.ds(n * C, C), :] = nt(left(final[n]), right_nt(s)).astype(BF16)
        s = nn(left(s), right_nn(passage[n]))
    high, low = split(s)
    sent[pl.ds(blocks * C, C), :] = high
    sent[pl.ds((blocks + 1) * C, C), :] = low


def transport(keys, house, rates):
    rows = keys.shape[0]
    blocks = rows // C
    square = jax.ShapeDtypeStruct((blocks, C, C), F32)
    flat = jax.ShapeDtypeStruct((rows, C), F32)
    return pl.pallas_call(
        transport_kernel,
        out_shape=(jax.ShapeDtypeStruct((rows + 2 * C, C), BF16), square, square, square, flat, flat),
        compiler_params=pltpu.CompilerParams(vmem_limit_bytes=VMEM_LIMIT),
        name="transport",
    )(keys, house, rates)


def own_kernel(
    queries, keys, values, passages, inverses, rights, finals, unit, moved, peak, total, summed, table, moving
):
    blocks = passages.shape[0]
    row = lax.broadcasted_iota(jnp.int32, (C, C), 0)
    col = lax.broadcasted_iota(jnp.int32, (C, C), 1)
    for n in range(blocks):
        here = pl.ds(n * C, C)
        q = queries[here, :].astype(F32) * (C**-0.5 * LOG2E)
        w = unit[here, :]
        k = keys[here, :]
        ql = left(q)
        seen = left(jnp.where(row >= col, nt(ql, right_nt(w)), 0.0))
        start = q - nn(left(nn(seen, right_nn(inverses[n]))), right_nn(w))
        inside = contract_last(ql, jnp.concatenate([k, k], axis=1)) - nt(seen, right_nt(rights[n]))
        table[here, here] = jnp.where(row >= col, inside, NEGATIVE)
        moving[here, :] = left(start)
    for m in range(blocks - 2, -1, -1):
        here = pl.ds(m * C, C)
        after = pl.ds((m + 1) * C, (blocks - 1 - m) * C)
        rows = moving[after, :]
        table[after, here] = nt(rows, right_nt(finals[here, :]))
        moving[after, :] = left(nn(rows, right_nn(passages[m])))
    moved[...] = moving[...]
    for n in range(blocks):
        here = pl.ds(n * C, C)
        upto = pl.ds(0, (n + 1) * C)
        s = table[here, upto]
        m = jnp.max(s, axis=1, keepdims=True)
        p = jnp.exp2(s - m)
        peak[here, :] = jnp.broadcast_to(m, (C, C))
        total[here, :] = jnp.broadcast_to(jnp.sum(p, axis=1, keepdims=True), (C, C))
        summed[here, :] = jnp.dot(p.astype(BF16), values[upto, :], preferred_element_type=F32)


def own(queries, keys, values, passages, inverses, rights, finals, unit):
    rows = queries.shape[0]
    flat = jax.ShapeDtypeStruct((rows, C), F32)
    return pl.pallas_call(
        own_kernel,
        out_shape=(jax.ShapeDtypeStruct((rows, 2 * C), BF16), flat, flat, flat),
        scratch_shapes=[pltpu.VMEM((rows, rows), F32), pltpu.VMEM((rows, 2 * C), BF16)],
        compiler_params=pltpu.CompilerParams(vmem_limit_bytes=VMEM_LIMIT),
        name="own",
    )(queries, keys, values, passages, inverses, rights, finals, unit)


ROWS = 256


def earlier_kernel(number, moved, peak, total, summed, all_keys, all_values, out, mv, mx, ls, acc):
    rows = moved.shape[0]
    mv[...] = moved[...]
    mx[...] = peak[...]
    ls[...] = total[...]
    acc[...] = summed[...]
    here_number = number[0]

    def visit(step, carry):
        source = here_number - 1 - step
        k = all_keys[source, pl.ds(0, rows), :]
        k2 = jnp.concatenate([k, k], axis=1)
        v = all_values[source]
        high = all_keys[source, pl.ds(rows, C), :]
        low = all_keys[source, pl.ds(rows + C, C), :]
        pair = jnp.concatenate([high, low], axis=1)
        step_by = jnp.concatenate([pair, pair], axis=0)
        for b in range(rows // ROWS):
            here = pl.ds(b * ROWS, ROWS)
            q = mv[here, :]
            s = contract_last(q, k2)
            mv[here, :] = left(nn(q, step_by))
            old = mx[here, :]
            new = jnp.maximum(old, jnp.max(s, axis=1, keepdims=True))
            mx[here, :] = new
            shrink = jnp.exp2(old - new)
            p = jnp.exp2(s - jnp.tile(new, (1, rows // C)))
            ls[here, :] = ls[here, :] * shrink + jnp.sum(p, axis=1, keepdims=True)
            acc[here, :] = acc[here, :] * shrink + jnp.dot(p.astype(BF16), v, preferred_element_type=F32)
        return carry

    lax.fori_loop(0, here_number, visit, 0)
    out[...] = (acc[...] / ls[...]).astype(BF16)


def earlier(number, moved, peak, total, summed, all_keys, all_values):
    rows = moved.shape[0]
    vmem = pl.BlockSpec(memory_space=pltpu.VMEM)
    return pl.pallas_call(
        earlier_kernel,
        out_shape=jax.ShapeDtypeStruct((rows, C), BF16),
        in_specs=[pl.BlockSpec(memory_space=pltpu.SMEM)] + [vmem] * 6,
        out_specs=vmem,
        scratch_shapes=[
            pltpu.VMEM((rows, 2 * C), BF16),
            pltpu.VMEM((rows, C), F32),
            pltpu.VMEM((rows, C), F32),
            pltpu.VMEM((rows, C), F32),
        ],
        compiler_params=pltpu.CompilerParams(vmem_limit_bytes=VMEM_LIMIT),
        name="earlier",
    )(number, moved, peak, total, summed, all_keys, all_values)


def over_heads(x):
    by_z = [lax.ppermute(x, "head", [(i, (i + 2 * s) % 8) for i in range(8)]) for s in (1, 3, 2)]
    return by_z


def body(queries, keys, values, house, rates, out_weight):
    rows = queries.shape[0]
    blocks = rows // C
    number = lax.axis_index("ctx")
    q, k, v, h = (x[:, 0, :] for x in (queries, keys, values, house))
    sent, passages, inverses, rights, finals, unit = transport(k, h, rates.reshape(blocks, C))
    all_values = lax.all_gather(v, "ctx", axis=0)
    all_keys = lax.all_gather(sent, "ctx", axis=0)
    moved, peak, total, summed = own(q, k, v, passages, inverses, rights, finals, unit)
    attended = earlier(number.astype(jnp.int32)[None], moved, peak, total, summed, all_keys, all_values)
    columns = lax.all_to_all(out_weight, "head", split_axis=1, concat_axis=0, tiled=True)
    everyone = lax.all_to_all(
        jnp.broadcast_to(attended[None], (8, *attended.shape)), "head", 0, 0, tiled=True
    )
    flattened = jnp.moveaxis(everyone, 0, 1).reshape(rows, 8 * C)
    projected = jnp.dot(flattened, columns, preferred_element_type=F32)
    return (attended[:, None, :], projected.astype(BF16))


def solution(mesh):
    in_specs = (
        P("ctx", "head", None),
        P("ctx", "head", None),
        P("ctx", "head", None),
        P("ctx", "head", None),
        P("head", "ctx"),
        P("head", None),
    )
    out_specs = (P("ctx", "head", None), P("ctx", "head"))
    return jax.shard_map(body, mesh=mesh, in_specs=in_specs, out_specs=out_specs, check_vma=False)
```

time: 471 us -> 200 us (0.42); the launches traced: 463 us -> 199 us
  matrix products: 161 us -> 3.49 us
  other arithmetic: 114 us -> 0 us
  Pallas kernels: 0 us -> 50.9 us
  local copies, waits for them, and re-layouts: 56.7 us -> 7.04 us
  loops' own time: 46.8 us -> 0 us
  waiting for transfers between devices: 53.4 us -> 86.7 us
  blocking collectives: 0 us -> 31.7 us
  starting transfers between devices: 17.4 us -> 5.39 us
    dot_general x109 -> x1, matrix products: 160 us -> 3.49 us  [body(): projected = jnp.dot(flattened, columns, preferred_element_type=F32)]
    another operation x1 -> x0, other arithmetic: 79.4 us -> none  [block_parts(): jax.scipy.linalg.solve_triangular(lower_part, identity, lower=True)]
    all_gather x2, waiting for transfers between devices: 25 us -> 86 us  [the longest x1 58.2 us: body(): all_keys = lax.all_gather(sent, 'ctx', axis=0)]
    pallas_call x0 -> x3, Pallas kernels: none -> 50.9 us  [the longest x1 36.1 us: earlier(): pl.pallas_call(earlier_kernel, out_shape=jax.ShapeDtypeStruct((rows, C),...]
    another operation x3 -> x0, loops' own time: 46.8 us -> none  [the longest x1 32.1 us: body(): lax.scan(through, running, (key_piece.reshape(groups, rows_dev, features)...]
    all_to_all x0 -> x1, blocking collectives: none -> 31.7 us  [body(): lax.all_to_all(jnp.broadcast_to(attended[None], (8, *attended.shape)), 'h...]
    all_to_all x2 -> x0, waiting for transfers between devices: 27.6 us -> none  [from_everyone(): lax.all_to_all(jnp.broadcast_to(x[None], (count, *x.shape)), axis, 0, 0,...]
    dynamic_slice x48 -> x0, local copies, waits for them, and re-layouts: 23.8 us -> none  [the longest x32 18.6 us: transfer_table(): lax.scan(gradient_pass, jnp.eye(features, dtype=all_ends.dtype), (sources...]
  transfers between devices with their start and end apart: 5 -> 3, of which waited for: 3 -> 2; matrix products, arithmetic and copies ran while one was open for 40% -> 3% of each run, Pallas kernels for 0% -> 26%
where the time goes in v1:
time: 200 us; the launch traced here: 199 us
  waiting for transfers between devices  86.7 us (43%)
  Pallas kernels  50.9 us (25%)
  blocking collectives  31.7 us (16%)
  between operations  14.1 us (7%)
  local copies, waits for them, and re-layouts  7.04 us (4%)
  starting transfers between devices  5.39 us (3%)
  matrix products  3.49 us (2%)
    all_gather x1, waiting for transfers between devices, body(): all_keys = lax.all_gather(sent, 'ctx', axis=0)  58.2 us
    pallas_call x1, Pallas kernels, earlier(): pl.pallas_call(earlier_kernel, out_shape=jax.ShapeDtypeStruct((rows, C),...  36.1 us
    all_to_all x1, blocking collectives, body(): lax.all_to_all(jnp.broadcast_to(attended[None], (8, *attended.shape)), 'h...  31.7 us
    all_gather x1, waiting for transfers between devices, body(): all_values = lax.all_gather(v, 'ctx', axis=0)  27.8 us
    pallas_call x1, Pallas kernels, transport(): pl.pallas_call(transport_kernel, out_shape=(jax.ShapeDtypeStruct((rows +...  8.19 us
    pallas_call x1, Pallas kernels, own(): pl.pallas_call(own_kernel, out_shape=(jax.ShapeDtypeStruct((rows, 2 * C),...  6.61 us
    all_to_all x1, starting transfers between devices, body(): lax.all_to_all(out_weight, 'head', split_axis=1, concat_axis=0, tiled=True)  5.31 us
  transfers between devices with their start and end apart: 3, of which 2 were waited for; matrix products, arithmetic and copies ran while one was open for 3% of the time, Pallas kernels for 26%

profile of v1, /device:TPU:30, one launch (start us, length us, event | category | flops | bytes accessed | tf_op | source)
XLA Modules:
  0.0 199.3 jit_solution(16671607694462154306)
XLA Ops:
  7.2 0.0 all-gather.7.cloned.1.call-start
  7.2 0.7 all-gather.7.cloned.1.call-update
  7.9 0.0 all-gather.5.cloned.1.call-start
  7.9 8.2 %transport.1 = (bf16[1280,128]{1,0:T(8,128)(2,1)}, f32[8,128,128]{2,1,0:T(8,128)}, f32[8,128,128]{2,1,0:T(8,128)}, f32[8,128,128]{2,1,0:T(8,128)}, f32[1024,128]{1,0:T(8,128)}, /*index=5*/f32[1024,128]{1,0:T(8,128)}) custom-call(bf16[1024,128]{1,0:T(8,128)(2,1)} %bitcast.22, bf16[1024,128]{1,0:T(8,128)(2,1)} %bitcast.25, f32[8,128]{1,0:T(8,128)} %bitcast.27), custom_call_target="tpu_custom_call" | custom-call | tf_op jit(solution)/shard_map/transport/pallas_call | solution.py:113
  16.1 0.0 all-gather.5.cloned.1.call-update
  16.2 3.2 %copy.8 = bf16[128,8192]{0,1:T(8,128)(2,1)S(1)} copy(bf16[128,8192]{1,0:T(8,128)(2,1)} %param.11) | data formatting | bytes 4194304 | tf_op args[5]
  19.4 2.6 %copy.9 = bf16[128,8,1024]{2,0,1:T(8,128)(2,1)} copy(bf16[128,8,1024]{0,2,1:T(8,128)(2,1)S(1)} %bitcast.18) | data formatting | bytes 4194304 | tf_op jit(solution)/shard_map/all_to_all | solution.py:240
  22.0 5.3 %all-to-all-start.1 = ((bf16[128,8,1024]{2,0,1:T(8,128)(2,1)}), bf16[128,8,1024]{2,0,1:T(8,128)(2,1)S(1)}, u32[]{:S(2)}, u32[]{:S(2)}) async-start(bf16[128,8,1024]{2,0,1:T(8,128)(2,1)} %copy.9), calls=%async_computation.1 | async-start | bytes 4194304 | tf_op jit(solution)/shard_map/all_to_all | solution.py:240
  27.3 6.6 %own.1 = (bf16[1024,256]{1,0:T(8,128)(2,1)}, f32[1024,128]{1,0:T(8,128)}, f32[1024,128]{1,0:T(8,128)}, f32[1024,128]{1,0:T(8,128)}) custom-call(bf16[1024,128]{1,0:T(8,128)(2,1)} %bitcast.26, bf16[1024,128]{1,0:T(8,128)(2,1)} %bitcast.23, bf16[1024,128]{1,0:T(8,128)(2,1)} %bitcast.24, f32[8,128,128]{2,1,0:T(8,128)} %get-tuple-element.12.passages, ...), custom_call_target="tpu_custom_call" | custom-call | tf_op jit(solution)/shard_map/own/pallas_call | solution.py:159
  33.9 27.8 %all-gather.7.cloned.1.call-done = bf16[16384,1,128]{2,0,1:T(8,128)(2,1)} async-done(((bf16[1024,1,128]{2,0,1:T(8,128)(2,1)}), bf16[16384,1,128]{2,0,1:T(8,128)(2,1)}) %all-gather.7.cloned.1.call-update) | async-done | bytes 4194320 | tf_op jit(solution)/shard_map/all_gather | solution.py:236
  61.7 58.2 %all-gather.5.cloned.1.call-done = bf16[20480,128]{1,0:T(8,128)(2,1)} async-done(((bf16[1280,128]{1,0:T(8,128)(2,1)}), bf16[20480,128]{1,0:T(8,128)(2,1)}) %all-gather.5.cloned.1.call-update) | async-done | bytes 5242896 | tf_op jit(solution)/shard_map/all_gather | solution.py:237
  119.9 36.1 %earlier.1 = bf16[1024,128]{1,0:T(8,128)(2,1)} custom-call(s32[1]{0:T(128)} %bitcast.number, bf16[1024,256]{1,0:T(8,128)(2,1)} %get-tuple-element.17.moved, f32[1024,128]{1,0:T(8,128)} %get-tuple-element.18.peak, f32[1024,128]{1,0:T(8,128)} %get-tuple-element.19.total, f32[1024,128]{1,0:T(8,128)} %get-tuple-element.20.summed, ...), custom_call_target="tpu_custom_call" | custom-call | tf_op jit(solution)/shard_map/earlier/pallas_call | solution.py:209
  156.0 0.0 all-to-all-done.1
  156.0 1.2 broadcast_in_dim.14
  157.2 31.7 %all_to_all.21 = bf16[8,1024,128]{2,1,0:T(8,128)(2,1)S(1)} all-to-all(bf16[8,1024,128]{2,1,0:T(8,128)(2,1)S(1)} %broadcast_in_dim.14), channel_id=1, replica_groups=mesh['head'=8,'ctx'=16] {'head'}, dimensions={0} | all-to-all | bytes 4194304 | tf_op jit(solution)/shard_map/all_to_all | solution.py:241
  188.9 3.5 %bitcast_convert_fusion = bf16[1024,1024]{1,0:T(8,128)(2,1)} fusion(bf16[128,8,1024]{2,0,1:T(8,128)(2,1)S(1)} %all-to-all-done.1, bf16[8,1024,128]{2,1,0:T(8,128)(2,1)S(1)} %all_to_all.21), kind=kOutput, calls=%fused_computation | convolution fusion | flops 2148532224 | bytes 6291456 | tf_op jit(solution)/shard_map/dot_general | solution.py:245
Async XLA Ops:
  7.2 54.6 %all-gather.7.cloned.1.call-start = ((), (), s32[]{:S(2)}) async-start(), calls=%async_computation.3 | async-start | bytes 4456448 | tf_op jit(solution)/shard_map/all_gather | solution.py:236
  7.9 112.0 %all-gather.5.cloned.1.call-start = ((), (), s32[]{:S(2)}) async-start(), calls=%async_computation.2 | async-start | bytes 5570560 | tf_op jit(solution)/shard_map/all_gather | solution.py:237
  22.0 134.0 %all-to-all-start.1 = ((bf16[128,8,1024]{2,0,1:T(8,128)(2,1)}), bf16[128,8,1024]{2,0,1:T(8,128)(2,1)S(1)}, u32[]{:S(2)}, u32[]{:S(2)}) async-start(bf16[128,8,1024]{2,0,1:T(8,128)(2,1)} %copy.9), calls=%async_computation.1 | async-start | bytes 4194304 | tf_op jit(solution)/shard_map/all_to_all | solution.py:240
Sparse Core Ops, SparseCore 0:
  10.1 51.5 all-gather.6
  63.9 55.9 all-gather.4

commit v2 on v1

--- a/solution.py
+++ b/solution.py
@@ -166,25 +166,37 @@
 
 
 ROWS = 256
-
-
-def earlier_kernel(number, moved, peak, total, summed, all_keys, all_values, out, mv, mx, ls, acc):
-    rows = moved.shape[0]
-    mv[...] = moved[...]
-    mx[...] = peak[...]
-    ls[...] = total[...]
-    acc[...] = summed[...]
-    here_number = number[0]
+SIDE = 4
+LSE_ROWS = 32
+
+
+def stacked(pair):
+    return jnp.concatenate([pair, pair], axis=0)
+
+
+def fetch_row(y, keys, values, key_row, value_row, sems):
+    copies = []
+    for d in range(SIDE):
+        slot = lax.rem(y + (SIDE - d), SIDE)
+        copies.append(pltpu.make_async_copy(keys[d], key_row.at[slot], sems.at[0, d]))
+        copies.append(pltpu.make_async_copy(values[d], value_row.at[slot], sems.at[1, d]))
+    for copy in copies:
+        copy.start()
+    for copy in copies:
+        copy.wait()
+
+
+def visit_row(first, count, key_row, value_row, mv, mx, ls, acc):
+    rows = mv.shape[0]
 
     def visit(step, carry):
-        source = here_number - 1 - step
-        k = all_keys[source, pl.ds(0, rows), :]
+        source = first - step
+        k = key_row[source, pl.ds(0, rows), :]
         k2 = jnp.concatenate([k, k], axis=1)
-        v = all_values[source]
-        high = all_keys[source, pl.ds(rows, C), :]
-        low = all_keys[source, pl.ds(rows + C, C), :]
-        pair = jnp.concatenate([high, low], axis=1)
-        step_by = jnp.concatenate([pair, pair], axis=0)
+        v = value_row[source]
+        high = key_row[source, pl.ds(rows, C), :]
+        low = key_row[source, pl.ds(rows + C, C), :]
+        step_by = stacked(jnp.concatenate([high, low], axis=1))
         for b in range(rows // ROWS):
             here = pl.ds(b * ROWS, ROWS)
             q = mv[here, :]
@@ -199,51 +211,263 @@
             acc[here, :] = acc[here, :] * shrink + jnp.dot(p.astype(BF16), v, preferred_element_type=F32)
         return carry
 
-    lax.fori_loop(0, here_number, visit, 0)
-    out[...] = (acc[...] / ls[...]).astype(BF16)
-
-
-def earlier(number, moved, peak, total, summed, all_keys, all_values):
+    lax.fori_loop(0, count, visit, 0)
+
+
+def row_scratch(rows, tail):
+    return [
+        pltpu.VMEM((SIDE, rows + 2 * C, C), BF16),
+        pltpu.VMEM((SIDE, rows, C), BF16),
+        pltpu.SemaphoreType.DMA((2, SIDE)),
+        pltpu.VMEM((rows, 2 * C), BF16),
+    ] + tail
+
+
+ANY = pl.BlockSpec(memory_space=pl.ANY)
+SCALARS = pl.BlockSpec(memory_space=pltpu.SMEM)
+WHOLE = pl.BlockSpec(memory_space=pltpu.VMEM)
+
+
+def chain_kernel(place, k0, k1, k2, k3, out, steps, sems):
+    y = place[1]
+    rows = k0.shape[0] - 2 * C
+    copies = []
+    for d, k in enumerate((k0, k1, k2, k3)):
+        slot = lax.rem(y + (SIDE - d), SIDE)
+        copies.append(pltpu.make_async_copy(k.at[pl.ds(rows, 2 * C)], steps.at[slot], sems.at[d]))
+    for copy in copies:
+        copy.start()
+    for copy in copies:
+        copy.wait()
+    row = lax.broadcasted_iota(jnp.int32, (C, C), 0)
+    col = lax.broadcasted_iota(jnp.int32, (C, C), 1)
+
+    def pair(n):
+        return jnp.concatenate([steps[n, pl.ds(0, C), :], steps[n, pl.ds(C, C), :]], axis=1)
+
+    def advance(step, so_far):
+        return nn(left(so_far), stacked(pair(y - 1 - step)))
+
+    before = lax.fori_loop(0, y, advance, jnp.where(row == col, 1.0, 0.0).astype(F32))
+    out[pl.ds(0, C), :] = left(before)
+    whole = pair(SIDE - 1)
+    for n in range(SIDE - 2, -1, -1):
+        whole = left(nn(whole, stacked(pair(n))))
+    out[pl.ds(C, C), :] = whole
+
+
+def chain(place, keys):
+    return pl.pallas_call(
+        chain_kernel,
+        out_shape=jax.ShapeDtypeStruct((2 * C, 2 * C), BF16),
+        in_specs=[SCALARS] + [ANY] * SIDE,
+        out_specs=WHOLE,
+        scratch_shapes=[pltpu.VMEM((SIDE, 2 * C, C), BF16), pltpu.SemaphoreType.DMA((SIDE,))],
+        compiler_params=pltpu.CompilerParams(vmem_limit_bytes=VMEM_LIMIT),
+        name="chain",
+    )(place, *keys)
+
+
+def row_kernel(
+    place, moved, peak, total, summed, k0, k1, k2, k3, v0, v1, v2, v3, mx, ls, acc, key_row, value_row, sems, mv
+):
+    y = place[1]
+    mv[...] = moved[...]
+    mx[...] = peak[...]
+    ls[...] = total[...]
+    acc[...] = summed[...]
+
+    @pl.when(y > 0)
+    def _():
+        fetch_row(y, (k0, k1, k2, k3), (v0, v1, v2, v3), key_row, value_row, sems)
+        visit_row(y - 1, y, key_row, value_row, mv, mx, ls, acc)
+
+
+def row(place, moved, peak, total, summed, keys, values):
     rows = moved.shape[0]
-    vmem = pl.BlockSpec(memory_space=pltpu.VMEM)
-    return pl.pallas_call(
-        earlier_kernel,
+    flat = jax.ShapeDtypeStruct((rows, C), F32)
+    return pl.pallas_call(
+        row_kernel,
+        out_shape=(flat, flat, flat),
+        in_specs=[SCALARS] + [WHOLE] * 4 + [ANY] * (2 * SIDE),
+        out_specs=(WHOLE, WHOLE, WHOLE),
+        scratch_shapes=row_scratch(rows, []),
+        compiler_params=pltpu.CompilerParams(vmem_limit_bytes=VMEM_LIMIT),
+        name="row",
+    )(place, moved, peak, total, summed, *keys, *values)
+
+
+def visitor_kernel(*refs):
+    place, query, k0, k1, k2, k3, v0, v1, v2, v3 = refs[:10]
+    key_row, value_row, sems, mv, mx, ls, acc = refs[-7:]
+    out = refs[-8]
+    chains = refs[10:-8]
+    distance = len(chains)
+    y = place[1]
+    rows = mv.shape[0]
+
+    @pl.when(place[0] + distance < SIDE)
+    def _():
+        fetch_row(y, (k0, k1, k2, k3), (v0, v1, v2, v3), key_row, value_row, sems)
+        along = chains[-1][pl.ds(0, C), :]
+        for link in chains[-2::-1]:
+            along = left(nn(along, stacked(link[pl.ds(C, C), :])))
+        mv[...] = left(nn(query[...], stacked(along)))
+        mx[...] = jnp.full(mx.shape, NEGATIVE, F32)
+        ls[...] = jnp.zeros(ls.shape, F32)
+        acc[...] = jnp.zeros(acc.shape, F32)
+        visit_row(SIDE - 1, SIDE, key_row, value_row, mv, mx, ls, acc)
+        out[pl.ds(0, rows), :] = (acc[...] / ls[...]).astype(BF16)
+        lines = []
+        for n in range(rows // C):
+            here = pl.ds(n * C, C)
+            lines.append(jnp.transpose(mx[here, :] + jnp.log2(ls[here, :]))[0:1, :])
+        lse = jnp.concatenate(lines, axis=0)
+        high = lse.astype(BF16).astype(F32)
+        middle = (lse - high).astype(BF16).astype(F32)
+        low = lse - high - middle
+        out[pl.ds(rows, LSE_ROWS), :] = jnp.concatenate(
+            [high, middle, low, jnp.zeros_like(lse)], axis=0
+        ).astype(BF16)
+
+
+def visitor(place, query, keys, values, chains):
+    rows = query.shape[0]
+    return pl.pallas_call(
+        visitor_kernel,
+        out_shape=jax.ShapeDtypeStruct((rows + LSE_ROWS, C), BF16),
+        in_specs=[SCALARS, WHOLE] + [ANY] * (2 * SIDE) + [WHOLE] * len(chains),
+        out_specs=WHOLE,
+        scratch_shapes=row_scratch(rows, [pltpu.VMEM((rows, C), F32)] * 3),
+        compiler_params=pltpu.CompilerParams(vmem_limit_bytes=VMEM_LIMIT),
+        name="visitor",
+    )(place, query, *keys, *values, *chains)
+
+
+def merge_kernel(place, mx, ls, acc, r1, r2, r3, out):
+    rows = mx.shape[0]
+    lines = []
+    for d, r in enumerate((r1, r2, r3)):
+        tail = r[pl.ds(rows, LSE_ROWS), :].astype(F32)
+        blocks = rows // C
+        lse = tail[0:blocks] + tail[blocks : 2 * blocks] + tail[2 * blocks : 3 * blocks]
+        lines.append(jnp.where(place[0] > d, lse, NEGATIVE))
+    for n in range(rows // C):
+        here = pl.ds(n * C, C)
+        lse = [jnp.transpose(jnp.broadcast_to(line[n : n + 1, :], (C, C))) for line in lines]
+        top = mx[here, :]
+        for one in lse:
+            top = jnp.maximum(top, one)
+        share = jnp.exp2(mx[here, :] - top)
+        total = ls[here, :] * share
+        summed = acc[here, :] * share
+        for d, r in enumerate((r1, r2, r3)):
+            share = jnp.exp2(lse[d] - top)
+            total += share
+            summed += jnp.where(place[0] > d, share * r[here, :].astype(F32), 0.0)
+        out[here, :] = (summed / total).astype(BF16)
+
+
+def merge(place, mx, ls, acc, returned):
+    rows = mx.shape[0]
+    return pl.pallas_call(
+        merge_kernel,
         out_shape=jax.ShapeDtypeStruct((rows, C), BF16),
-        in_specs=[pl.BlockSpec(memory_space=pltpu.SMEM)] + [vmem] * 6,
-        out_specs=vmem,
-        scratch_shapes=[
-            pltpu.VMEM((rows, 2 * C), BF16),
-            pltpu.VMEM((rows, C), F32),
-            pltpu.VMEM((rows, C), F32),
-            pltpu.VMEM((rows, C), F32),
-        ],
-        compiler_params=pltpu.CompilerParams(vmem_limit_bytes=VMEM_LIMIT),
-        name="earlier",
-    )(number, moved, peak, total, summed, all_keys, all_values)
-
-
-def over_heads(x):
-    by_z = [lax.ppermute(x, "head", [(i, (i + 2 * s) % 8) for i in range(8)]) for s in (1, 3, 2)]
-    return by_z
+        in_specs=[SCALARS] + [WHOLE] * 6,
+        out_specs=WHOLE,
+        compiler_params=pltpu.CompilerParams(vmem_limit_bytes=VMEM_LIMIT),
+        name="merge",
+    )(place, mx, ls, acc, *returned)
+
+
+def project_kernel(place, here, there, columns, *rest):
+    out = rest[-1]
+    z, core = place[2], place[3]
+    total = None
+    for s in range(SIDE):
+        chip = lax.rem(z + (SIDE - s), SIDE)
+        x = jnp.concatenate([here[s], there[s]], axis=1)
+        w = jnp.concatenate([columns[2 * chip + core], columns[2 * chip + 1 - core]], axis=0)
+        part = jnp.dot(x, w, preferred_element_type=F32)
+        total = part if total is None else total + part
+    out[...] = total.astype(BF16)
+
+
+def project(place, here, there, columns, part, parts, so_far):
+    rows = here.shape[1]
+    width = columns.shape[2]
+    tile = 256
+    steps = rows // tile
+    extra = [] if so_far is None else [so_far]
+    piece = pl.BlockSpec((SIDE, tile, C), lambda i: (0, i, 0))
+    return pl.pallas_call(
+        project_kernel,
+        out_shape=jax.ShapeDtypeStruct((rows * parts, width), BF16),
+        grid=(steps,),
+        in_specs=[SCALARS, piece, piece, WHOLE] + [ANY] * len(extra),
+        out_specs=pl.BlockSpec((tile, width), lambda i: (part * steps + i, 0)),
+        input_output_aliases={4: 0} if extra else {},
+        compiler_params=pltpu.CompilerParams(vmem_limit_bytes=VMEM_LIMIT),
+        name="project",
+    )(place, here, there, columns, *extra)
+
+
+def along_y(x, d):
+    return lax.ppermute(x, "ctx", [(i, i - i % SIDE + (i + d) % SIDE) for i in range(SIDE * SIDE)])
+
+
+def down_x(x, d):
+    return lax.ppermute(x, "ctx", [(i, i - SIDE * d) for i in range(SIDE * d, SIDE * SIDE)])
+
+
+def up_x(x, d):
+    return lax.ppermute(x, "ctx", [(i, i + SIDE * d) for i in range(SIDE * SIDE - SIDE * d)])
+
+
+def along_z(x, d):
+    return lax.ppermute(x, "head", [(i, (i + 2 * d) % (2 * SIDE)) for i in range(2 * SIDE)])
+
+
+def other_core(x):
+    return lax.ppermute(x, "head", [(i, i ^ 1) for i in range(2 * SIDE)])
+
+
+PARTS = 2
 
 
 def body(queries, keys, values, house, rates, out_weight):
     rows = queries.shape[0]
     blocks = rows // C
     number = lax.axis_index("ctx")
+    head = lax.axis_index("head")
+    place = jnp.stack([number // SIDE, number % SIDE, head // 2, head % 2]).astype(jnp.int32)
     q, k, v, h = (x[:, 0, :] for x in (queries, keys, values, house))
+    row_values = [v] + [along_y(v, d) for d in (1, 2, 3)]
     sent, passages, inverses, rights, finals, unit = transport(k, h, rates.reshape(blocks, C))
-    all_values = lax.all_gather(v, "ctx", axis=0)
-    all_keys = lax.all_gather(sent, "ctx", axis=0)
+    row_keys = [sent] + [along_y(sent, d) for d in (1, 2, 3)]
     moved, peak, total, summed = own(q, k, v, passages, inverses, rights, finals, unit)
-    attended = earlier(number.astype(jnp.int32)[None], moved, peak, total, summed, all_keys, all_values)
+    visiting = [down_x(moved, d) for d in (1, 2, 3)]
+    links = chain(place, row_keys)
+    links = [down_x(links, d) for d in (1, 2, 3)]
+    mx, ls, acc = row(place, moved, peak, total, summed, row_keys, row_values)
+    returned = []
+    for d in (1, 2, 3):
+        partial = visitor(place, visiting[d - 1], row_keys, row_values, links[:d])
+        returned.append(up_x(partial, d))
+    attended = merge(place, mx, ls, acc, returned)
+    width = out_weight.shape[1] // (2 * SIDE)
     columns = lax.all_to_all(out_weight, "head", split_axis=1, concat_axis=0, tiled=True)
-    everyone = lax.all_to_all(
-        jnp.broadcast_to(attended[None], (8, *attended.shape)), "head", 0, 0, tiled=True
-    )
-    flattened = jnp.moveaxis(everyone, 0, 1).reshape(rows, 8 * C)
-    projected = jnp.dot(flattened, columns, preferred_element_type=F32)
-    return (attended[:, None, :], projected.astype(BF16))
+    columns = columns.reshape(2 * SIDE, C, width)
+    projected = None
+    pieces = []
+    for part in range(PARTS):
+        size = rows // PARTS
+        mine = attended[part * size : (part + 1) * size]
+        here = jnp.stack([mine] + [along_z(mine, d) for d in (1, 2, 3)])
+        pieces.append((here, other_core(here)))
+    for part, (here, there) in enumerate(pieces):
+        projected = project(place, here, there, columns, part, PARTS, projected)
+    return (attended[:, None, :], projected)
 
 
 def solution(mesh):

time: 200 us -> 155 us (0.78)
  the two profiles are of different devices: /device:TPU:30 before, /device:TPU:25 now
where the time goes in v2:
time: 155 us; the launch traced here: 154 us
  Pallas kernels  76.9 us (50%)
  starting transfers between devices  39.2 us (25%)
  waiting for transfers between devices  26.7 us (17%)
  local copies, waits for them, and re-layouts  9.74 us (6%)
    pallas_call x3, Pallas kernels, visitor(): pl.pallas_call(visitor_kernel, out_shape=jax.ShapeDtypeStruct((rows + LSE...  37.1 us
    ppermute x6, waiting for transfers between devices, along_y(): lax.ppermute(x, 'ctx', [(i, i - i % SIDE + (i + d) % SIDE) for i in range...  13.5 us
    pallas_call x1, Pallas kernels, row(): pl.pallas_call(row_kernel, out_shape=(flat, flat, flat), in_specs=[SCALAR...  10.7 us
    ppermute x6, waiting for transfers between devices, down_x(): lax.ppermute(x, 'ctx', [(i, i - SIDE * d) for i in range(SIDE * d, SIDE *...  9.84 us
    pallas_call x1, Pallas kernels, transport(): pl.pallas_call(transport_kernel, out_shape=(jax.ShapeDtypeStruct((rows +...  8.2 us
    pallas_call x2, Pallas kernels, project(): pl.pallas_call(project_kernel, out_shape=jax.ShapeDtypeStruct((rows * par...  8.12 us
    ppermute x6, starting transfers between devices, along_z(): lax.ppermute(x, 'head', [(i, (i + 2 * d) % (2 * SIDE)) for i in range(2 *...  8.1 us
    all_to_all x1, starting transfers between devices, body(): lax.all_to_all(out_weight, 'head', split_axis=1, concat_axis=0, tiled=True)  8.03 us
  transfers between devices with their start and end apart: 24, of which 9 were waited for; matrix products, arithmetic and copies ran while one was open for 5% of the time, Pallas kernels for 42%

profile of v2, /device:TPU:25, one launch (start us, length us, event | category | flops | bytes accessed | tf_op | source)
XLA Modules:
  0.0 154.3 jit_solution(4109086370197502488)
XLA Ops:
  0.6 8.2 %transport.1 = (bf16[1280,128]{1,0:T(8,128)(2,1)}, f32[8,128,128]{2,1,0:T(8,128)}, f32[8,128,128]{2,1,0:T(8,128)}, f32[8,128,128]{2,1,0:T(8,128)}, f32[1024,128]{1,0:T(8,128)}, /*index=5*/f32[1024,128]{1,0:T(8,128)}) custom-call(bf16[1024,128]{1,0:T(8,128)(2,1)} %bitcast.34, bf16[1024,128]{1,0:T(8,128)(2,1)} %bitcast.36, f32[8,128]{1,0:T(8,128)} %bitcast.44), custom_call_target="tpu_custom_call" | custom-call | tf_op jit(solution)/shard_map/transport/pallas_call | solution.py:113
  8.8 2.2 %collective-permute-start.1 = (bf16[1280,128]{1,0:T(8,128)(2,1)}, bf16[1280,128]{1,0:T(8,128)(2,1)S(1)}, u32[]{:S(2)}, u32[]{:S(2)}) collective-permute-start(bf16[1280,128]{1,0:T(8,128)(2,1)} %get-tuple-element.24.k0.refs_2_), channel_id=1, source_target_pairs={{0,2},{1,3},{2,0},{3,1},{4,6},{5,7},{6,4},{7,5},{8,10},{9,11},{10,... | collective-permute-start | bytes 983048 | tf_op jit(solution)/shard_map/ppermute | solution.py:416
  11.1 1.6 %collective-permute-start.3 = (bf16[1024,128]{1,0:T(8,128)(2,1)}, bf16[1024,128]{1,0:T(8,128)(2,1)S(1)}, u32[]{:S(2)}, u32[]{:S(2)}) collective-permute-start(bf16[1024,128]{1,0:T(8,128)(2,1)} %bitcast.25), channel_id=1, source_target_pairs={{0,1},{1,2},{2,3},{3,0},{4,5},{5,6},{6,7},{7,4},{8,9},{9,10},{10,1... | collective-permute-start | bytes 786440 | tf_op jit(solution)/shard_map/ppermute | solution.py:416
  13.9 6.7 %own.1 = (bf16[1024,256]{1,0:T(8,128)(2,1)}, f32[1024,128]{1,0:T(8,128)}, f32[1024,128]{1,0:T(8,128)}, f32[1024,128]{1,0:T(8,128)}) custom-call(bf16[1024,128]{1,0:T(8,128)(2,1)} %bitcast.37, bf16[1024,128]{1,0:T(8,128)(2,1)} %bitcast.35, bf16[1024,128]{1,0:T(8,128)(2,1)} %bitcast.27, f32[8,128,128]{2,1,0:T(8,128)} %get-tuple-element.15.passages, ...), custom_call_target="tpu_custom_call" | custom-call | tf_op jit(solution)/shard_map/own/pallas_call | solution.py:159
  20.5 9.9 %collective-permute-done.3.v1.refs_7_ = bf16[1024,128]{1,0:T(8,128)(2,1)S(1)} collective-permute-done((bf16[1024,128]{1,0:T(8,128)(2,1)}, bf16[1024,128]{1,0:T(8,128)(2,1)S(1)}, u32[]{:S(2)}, u32[]{:S(2)}) %collective-permute-start.3) | collective-permute-done | bytes 262176 | tf_op jit(solution)/shard_map/ppermute | solution.py:416
  34.3 3.2 %copy.9 = bf16[128,8192]{0,1:T(8,128)(2,1)S(1)} copy(bf16[128,8192]{1,0:T(8,128)(2,1)} %param.11) | data formatting | bytes 4194304 | tf_op args[5]
  37.6 2.6 %copy.10 = bf16[128,8,1024]{2,0,1:T(8,128)(2,1)} copy(bf16[128,8,1024]{0,2,1:T(8,128)(2,1)S(1)} %bitcast.24) | data formatting | bytes 4194304 | tf_op jit(solution)/shard_map/all_to_all | solution.py:459
  40.2 8.0 %all-to-all-start = ((bf16[128,8,1024]{2,0,1:T(8,128)(2,1)}), bf16[128,8,1024]{2,0,1:T(8,128)(2,1)S(1)}, u32[]{:S(2)}, u32[]{:S(2)}) async-start(bf16[128,8,1024]{2,0,1:T(8,128)(2,1)} %copy.10), calls=%async_computation | async-start | bytes 4194304 | tf_op jit(solution)/shard_map/all_to_all | solution.py:459
  49.4 3.2 %chain.1 = bf16[256,256]{1,0:T(8,128)(2,1)} custom-call(s32[4]{0:T(128)} %pad_add_fusion.place.refs_0_, bf16[1280,128]{1,0:T(8,128)(2,1)} %get-tuple-element.24.k0.refs_2_, bf16[1280,128]{1,0:T(8,128)(2,1)} %copy-done.1, bf16[1280,128]{1,0:T(8,128)(2,1)} %copy-done.2, bf16[1280,128]{1,0:T(8,128)(2,1)} %copy-done.3), custom_call_target="tpu_custom_call" | custom-call | tf_op jit(solution)/shard_map/chain/pallas_call | solution.py:260
  53.9 3.6 %collective-permute-done.5.v3.refs_9_ = bf16[1024,128]{1,0:T(8,128)(2,1)S(1)} collective-permute-done((bf16[1024,128]{1,0:T(8,128)(2,1)S(1)}, bf16[1024,128]{1,0:T(8,128)(2,1)S(1)}, u32[]{:S(2)}, u32[]{:S(2)}) %collective-permute-start.5) | collective-permute-done | bytes 262176 | tf_op jit(solution)/shard_map/ppermute | solution.py:416
  58.9 4.2 %collective-permute-done.10.refs_11_ = bf16[256,256]{1,0:T(8,128)(2,1)S(1)} collective-permute-done((bf16[256,256]{1,0:T(8,128)(2,1)}, bf16[256,256]{1,0:T(8,128)(2,1)S(1)}, u32[]{:S(2)}, u32[]{:S(2)}) %collective-permute-start.10) | collective-permute-done | bytes 131104 | tf_op jit(solution)/shard_map/ppermute | solution.py:420
  64.5 4.1 %collective-permute-done.13.refs_12_ = bf16[256,256]{1,0:T(8,128)(2,1)S(1)} collective-permute-done((bf16[256,256]{1,0:T(8,128)(2,1)}, bf16[256,256]{1,0:T(8,128)(2,1)S(1)}, u32[]{:S(2)}, u32[]{:S(2)}) %collective-permute-start.13) | collective-permute-done | bytes 131104 | tf_op jit(solution)/shard_map/ppermute | solution.py:420
  68.7 1.5 collective-permute-done.7.refs_10_
  70.8 12.5 %visitor.5 = bf16[1056,128]{1,0:T(8,128)(2,1)} custom-call(s32[4]{0:T(128)} %pad_add_fusion.place.refs_0_, bf16[1024,256]{1,0:T(8,128)(2,1)} %collective-permute-done.12.refs_1_, bf16[1280,128]{1,0:T(8,128)(2,1)} %get-tuple-element.24.k0.refs_2_, bf16[1280,128]{1,0:T(8,128)(2,1)} %copy-done.1, bf16[1280,128]{1,0:T(8,128)(2,1)} %copy-done.2, ...), custom_call_target="tpu_custom_call" | custom-call | tf_op jit(solution)/shard_map/visitor/pallas_call | solution.py:336
  84.7 12.4 %visitor.4 = bf16[1056,128]{1,0:T(8,128)(2,1)} custom-call(s32[4]{0:T(128)} %pad_add_fusion.place.refs_0_, bf16[1024,256]{1,0:T(8,128)(2,1)} %collective-permute-done.9.refs_1_, bf16[1280,128]{1,0:T(8,128)(2,1)} %get-tuple-element.24.k0.refs_2_, bf16[1280,128]{1,0:T(8,128)(2,1)} %copy-done.1, bf16[1280,128]{1,0:T(8,128)(2,1)} %copy-done.2, ...), custom_call_target="tpu_custom_call" | custom-call | tf_op jit(solution)/shard_map/visitor/pallas_call | solution.py:336
  98.4 12.2 %visitor.3 = bf16[1056,128]{1,0:T(8,128)(2,1)} custom-call(s32[4]{0:T(128)} %pad_add_fusion.place.refs_0_, bf16[1024,256]{1,0:T(8,128)(2,1)} %collective-permute-done.6.refs_1_, bf16[1280,128]{1,0:T(8,128)(2,1)} %get-tuple-element.24.k0.refs_2_, bf16[1280,128]{1,0:T(8,128)(2,1)} %copy-done.1, bf16[1280,128]{1,0:T(8,128)(2,1)} %copy-done.2, ...), custom_call_target="tpu_custom_call" | custom-call | tf_op jit(solution)/shard_map/visitor/pallas_call | solution.py:336
  111.9 10.7 %row.1 = (f32[1024,128]{1,0:T(8,128)}, f32[1024,128]{1,0:T(8,128)}, f32[1024,128]{1,0:T(8,128)}) custom-call(s32[4]{0:T(128)} %pad_add_fusion.place.refs_0_, bf16[1024,256]{1,0:T(8,128)(2,1)} %get-tuple-element.20.moved, f32[1024,128]{1,0:T(8,128)} %get-tuple-element.21.peak, f32[1024,128]{1,0:T(8,128)} %get-tuple-element.22.total, ...), custom_call_target="tpu_custom_call" | custom-call | tf_op jit(solution)/shard_map/row/pallas_call | solution.py:289
  123.5 2.9 %merge.1 = bf16[1024,128]{1,0:T(8,128)(2,1)} custom-call(s32[4]{0:T(128)} %pad_add_fusion.place.refs_0_, f32[1024,128]{1,0:T(8,128)} %get-tuple-element.25.mx, f32[1024,128]{1,0:T(8,128)} %get-tuple-element.26.ls, f32[1024,128]{1,0:T(8,128)} %get-tuple-element.27.acc, bf16[1056,128]{1,0:T(8,128)(2,1)} %copy-done.13, bf16[1056,128]{1,0:T(8,128)(2,1)} %copy-done.12, ...), custom_call_target="tpu_custom_call" | custom-call | tf_op jit(solution)/shard_map/merge/pallas_call | solution.py:373
  128.1 3.6 %collective-permute-start.20 = (bf16[512,128]{1,0:T(8,128)(2,1)S(1)}, bf16[512,128]{1,0:T(8,128)(2,1)S(1)}, u32[]{:S(2)}, u32[]{:S(2)}) collective-permute-start(bf16[512,128]{1,0:T(8,128)(2,1)S(1)} %get-tuple-element.30), channel_id=1, source_target_pairs={{0,64},{16,80},{32,96},{48,112},{64,0},{80,16},{96,32},{112,48},{1... | collective-permute-start | bytes 393224 | tf_op jit(solution)/shard_map/ppermute | solution.py:428
  133.2 2.4 %collective-permute-start.17 = (bf16[512,128]{1,0:T(8,128)(2,1)S(1)}, bf16[512,128]{1,0:T(8,128)(2,1)S(1)}, u32[]{:S(2)}, u32[]{:S(2)}) collective-permute-start(bf16[512,128]{1,0:T(8,128)(2,1)S(1)} %get-tuple-element.31), channel_id=1, source_target_pairs={{0,96},{16,112},{32,0},{48,16},{64,32},{80,48},{96,64},{112,80},{1... | collective-permute-start | bytes 393224 | tf_op jit(solution)/shard_map/ppermute | solution.py:428
  137.3 3.9 %collective-permute-start.22 = (bf16[4,512,128]{2,1,0:T(8,128)(2,1)S(1)}, bf16[4,512,128]{2,1,0:T(8,128)(2,1)}, u32[]{:S(2)}, u32[]{:S(2)}) collective-permute-start(bf16[4,512,128]{2,1,0:T(8,128)(2,1)S(1)} %pad_maximum_fusion.1.here), channel_id=1, source_target_pairs={{0,16},{16,0},{32,48},{48,32},{64,80},{80,64},{96,112},{112,96},{1... | collective-permute-start | bytes 1572872 | tf_op jit(solution)/shard_map/ppermute | solution.py:432
  142.9 1.9 %collective-permute-start.18 = (bf16[4,512,128]{2,1,0:T(8,128)(2,1)S(1)}, bf16[4,512,128]{2,1,0:T(8,128)(2,1)}, u32[]{:S(2)}, u32[]{:S(2)}) collective-permute-start(bf16[4,512,128]{2,1,0:T(8,128)(2,1)S(1)} %pad_maximum_fusion.here), channel_id=1, source_target_pairs={{0,16},{16,0},{32,48},{48,32},{64,80},{80,64},{96,112},{112,96},{1... | collective-permute-start | bytes 1572872 | tf_op jit(solution)/shard_map/ppermute | solution.py:432
  146.2 4.0 %project.2.rest_0_ = bf16[1024,1024]{1,0:T(8,128)(2,1)} custom-call(s32[4]{0:T(128)} %pad_add_fusion.place.refs_0_, bf16[4,512,128]{2,1,0:T(8,128)(2,1)} %copy-done.7, bf16[4,512,128]{2,1,0:T(8,128)(2,1)} %collective-permute-done.22.there, bf16[8,128,1024]{2,1,0:T(8,128)(2,1)} %bitcast.22), custom_call_target="tpu_custom_call" | custom-call | tf_op jit(solution)/shard_map/project/pallas_call | solution.py:403
  150.2 4.1 %project.3 = bf16[1024,1024]{1,0:T(8,128)(2,1)} custom-call(s32[4]{0:T(128)} %pad_add_fusion.place.refs_0_, bf16[4,512,128]{2,1,0:T(8,128)(2,1)} %copy-done.8, bf16[4,512,128]{2,1,0:T(8,128)(2,1)} %collective-permute-done.18.there, bf16[8,128,1024]{2,1,0:T(8,128)(2,1)} %bitcast.23, bf16[1024,1024]{1,0:T(8,128)(2,1)} %project.2.rest_0_), custom_call_target="tpu_custom_call", output_to_operand_aliasing={{}: (4, {})} | custom-call | tf_op jit(solution)/shard_map/project/pallas_call | solution.py:403
  (70 shorter events, 23.6 us)
Async XLA Ops:
  8.8 22.9 %collective-permute-start = (bf16[1280,128]{1,0:T(8,128)(2,1)}, bf16[1280,128]{1,0:T(8,128)(2,1)S(1)}, u32[]{:S(2)}, u32[]{:S(2)}) collective-permute-start(bf16[1280,128]{1,0:T(8,128)(2,1)} %get-tuple-element.24.k0.refs_2_), channel_id=1, source_target_pairs={{0,1},{1,2},{2,3},{3,0},{4,5},{5,6},{6,7},{7,4},{8,9},{9,10},{10,1... | collective-permute-start | bytes 983048 | tf_op jit(solution)/shard_map/ppermute | solution.py:416
  8.8 24.2 %collective-permute-start.1 = (bf16[1280,128]{1,0:T(8,128)(2,1)}, bf16[1280,128]{1,0:T(8,128)(2,1)S(1)}, u32[]{:S(2)}, u32[]{:S(2)}) collective-permute-start(bf16[1280,128]{1,0:T(8,128)(2,1)} %get-tuple-element.24.k0.refs_2_), channel_id=1, source_target_pairs={{0,2},{1,3},{2,0},{3,1},{4,6},{5,7},{6,4},{7,5},{8,10},{9,11},{10,... | collective-permute-start | bytes 983048 | tf_op jit(solution)/shard_map/ppermute | solution.py:416
  11.1 19.3 %collective-permute-start.3 = (bf16[1024,128]{1,0:T(8,128)(2,1)}, bf16[1024,128]{1,0:T(8,128)(2,1)S(1)}, u32[]{:S(2)}, u32[]{:S(2)}) collective-permute-start(bf16[1024,128]{1,0:T(8,128)(2,1)} %bitcast.25), channel_id=1, source_target_pairs={{0,1},{1,2},{2,3},{3,0},{4,5},{5,6},{6,7},{7,4},{8,9},{9,10},{10,1... | collective-permute-start | bytes 786440 | tf_op jit(solution)/shard_map/ppermute | solution.py:416
  12.7 35.5 %collective-permute-start.2 = (bf16[1280,128]{1,0:T(8,128)(2,1)}, bf16[1280,128]{1,0:T(8,128)(2,1)S(1)}, u32[]{:S(2)}, u32[]{:S(2)}) collective-permute-start(bf16[1280,128]{1,0:T(8,128)(2,1)} %get-tuple-element.24.k0.refs_2_), channel_id=1, source_target_pairs={{0,3},{1,0},{2,1},{3,2},{4,7},{5,4},{6,5},{7,6},{8,11},{9,8},{10,9... | collective-permute-start | bytes 983048 | tf_op jit(solution)/shard_map/ppermute | solution.py:416
  12.7 39.9 %collective-permute-start.4 = (bf16[1024,128]{1,0:T(8,128)(2,1)}, bf16[1024,128]{1,0:T(8,128)(2,1)}, u32[]{:S(2)}, u32[]{:S(2)}) collective-permute-start(bf16[1024,128]{1,0:T(8,128)(2,1)} %bitcast.26), channel_id=1, source_target_pairs={{0,2},{1,3},{2,0},{3,1},{4,6},{5,7},{6,4},{7,5},{8,10},{9,11},{10,... | collective-permute-start | bytes 786440 | tf_op jit(solution)/shard_map/ppermute | solution.py:416
  30.4 39.8 %collective-permute-start.12 = (bf16[1024,256]{1,0:T(8,128)(2,1)}, bf16[1024,256]{1,0:T(8,128)(2,1)}, u32[]{:S(2)}, u32[]{:S(2)}) collective-permute-start(bf16[1024,256]{1,0:T(8,128)(2,1)} %get-tuple-element.20.moved), channel_id=1, source_target_pairs={{12,0},{13,1},{14,2},{15,3},{28,16},{29,17},{30,18},{31,19},{44,32... | collective-permute-start | bytes 1572872 | tf_op jit(solution)/shard_map/ppermute | solution.py:420
  31.7 53.0 %collective-permute-start.9 = (bf16[1024,256]{1,0:T(8,128)(2,1)}, bf16[1024,256]{1,0:T(8,128)(2,1)}, u32[]{:S(2)}, u32[]{:S(2)}) collective-permute-start(bf16[1024,256]{1,0:T(8,128)(2,1)} %get-tuple-element.20.moved), channel_id=1, source_target_pairs={{8,0},{9,1},{10,2},{11,3},{12,4},{13,5},{14,6},{15,7},{24,16},{25,... | collective-permute-start | bytes 1572872 | tf_op jit(solution)/shard_map/ppermute | solution.py:420
  33.0 65.4 %collective-permute-start.6 = (bf16[1024,256]{1,0:T(8,128)(2,1)}, bf16[1024,256]{1,0:T(8,128)(2,1)}, u32[]{:S(2)}, u32[]{:S(2)}) collective-permute-start(bf16[1024,256]{1,0:T(8,128)(2,1)} %get-tuple-element.20.moved), channel_id=1, source_target_pairs={{4,0},{5,1},{6,2},{7,3},{8,4},{9,5},{10,6},{11,7},{12,8},{13,9},{1... | collective-permute-start | bytes 1572872 | tf_op jit(solution)/shard_map/ppermute | solution.py:420
  40.2 104.6 %all-to-all-start = ((bf16[128,8,1024]{2,0,1:T(8,128)(2,1)}), bf16[128,8,1024]{2,0,1:T(8,128)(2,1)S(1)}, u32[]{:S(2)}, u32[]{:S(2)}) async-start(bf16[128,8,1024]{2,0,1:T(8,128)(2,1)} %copy.10), calls=%async_computation | async-start | bytes 4194304 | tf_op jit(solution)/shard_map/all_to_all | solution.py:459
  48.3 9.3 %collective-permute-start.5 = (bf16[1024,128]{1,0:T(8,128)(2,1)S(1)}, bf16[1024,128]{1,0:T(8,128)(2,1)S(1)}, u32[]{:S(2)}, u32[]{:S(2)}) collective-permute-start(bf16[1024,128]{1,0:T(8,128)(2,1)S(1)} %bitcast.32), channel_id=1, source_target_pairs={{0,3},{1,0},{2,1},{3,2},{4,7},{5,4},{6,5},{7,6},{8,11},{9,8},{10,9... | collective-permute-start | bytes 786440 | tf_op jit(solution)/shard_map/ppermute | solution.py:416
  52.6 10.4 %collective-permute-start.10 = (bf16[256,256]{1,0:T(8,128)(2,1)}, bf16[256,256]{1,0:T(8,128)(2,1)S(1)}, u32[]{:S(2)}, u32[]{:S(2)}) collective-permute-start(bf16[256,256]{1,0:T(8,128)(2,1)} %chain.1), channel_id=1, source_target_pairs={{8,0},{9,1},{10,2},{11,3},{12,4},{13,5},{14,6},{15,7},{24,16},{25,... | collective-permute-start | bytes 393224 | tf_op jit(solution)/shard_map/ppermute | solution.py:420
  57.6 11.1 %collective-permute-start.13 = (bf16[256,256]{1,0:T(8,128)(2,1)}, bf16[256,256]{1,0:T(8,128)(2,1)S(1)}, u32[]{:S(2)}, u32[]{:S(2)}) collective-permute-start(bf16[256,256]{1,0:T(8,128)(2,1)} %chain.1), channel_id=1, source_target_pairs={{12,0},{13,1},{14,2},{15,3},{28,16},{29,17},{30,18},{31,19},{44,32... | collective-permute-start | bytes 393224 | tf_op jit(solution)/shard_map/ppermute | solution.py:420
  63.0 7.1 %collective-permute-start.7 = (bf16[256,256]{1,0:T(8,128)(2,1)}, bf16[256,256]{1,0:T(8,128)(2,1)S(1)}, u32[]{:S(2)}, u32[]{:S(2)}) collective-permute-start(bf16[256,256]{1,0:T(8,128)(2,1)} %chain.1), channel_id=1, source_target_pairs={{4,0},{5,1},{6,2},{7,3},{8,4},{9,5},{10,6},{11,7},{12,8},{13,9},{1... | collective-permute-start | bytes 393224 | tf_op jit(solution)/shard_map/ppermute | solution.py:420
  83.4 39.2 %collective-permute-start.14 = (bf16[1056,128]{1,0:T(8,128)(2,1)}, bf16[1056,128]{1,0:T(8,128)(2,1)S(1)}, u32[]{:S(2)}, u32[]{:S(2)}) collective-permute-start(bf16[1056,128]{1,0:T(8,128)(2,1)} %visitor.5), channel_id=1, source_target_pairs={{0,12},{1,13},{2,14},{3,15},{16,28},{17,29},{18,30},{19,31},{32,44... | collective-permute-start | bytes 811016 | tf_op jit(solution)/shard_map/ppermute | solution.py:424
  97.1 25.5 %collective-permute-start.11 = (bf16[1056,128]{1,0:T(8,128)(2,1)}, bf16[1056,128]{1,0:T(8,128)(2,1)S(1)}, u32[]{:S(2)}, u32[]{:S(2)}) collective-permute-start(bf16[1056,128]{1,0:T(8,128)(2,1)} %visitor.4), channel_id=1, source_target_pairs={{0,8},{1,9},{2,10},{3,11},{4,12},{5,13},{6,14},{7,15},{16,24},{17,... | collective-permute-start | bytes 811016 | tf_op jit(solution)/shard_map/ppermute | solution.py:424
  110.6 12.0 %collective-permute-start.8 = (bf16[1056,128]{1,0:T(8,128)(2,1)}, bf16[1056,128]{1,0:T(8,128)(2,1)S(1)}, u32[]{:S(2)}, u32[]{:S(2)}) collective-permute-start(bf16[1056,128]{1,0:T(8,128)(2,1)} %visitor.3), channel_id=1, source_target_pairs={{0,4},{1,5},{2,6},{3,7},{4,8},{5,9},{6,10},{7,11},{8,12},{9,13},{1... | collective-permute-start | bytes 811016 | tf_op jit(solution)/shard_map/ppermute | solution.py:424
  127.5 5.7 %collective-permute-start.19 = (bf16[512,128]{1,0:T(8,128)(2,1)S(1)}, bf16[512,128]{1,0:T(8,128)(2,1)S(1)}, u32[]{:S(2)}, u32[]{:S(2)}) collective-permute-start(bf16[512,128]{1,0:T(8,128)(2,1)S(1)} %get-tuple-element.30), channel_id=1, source_target_pairs={{0,32},{16,48},{32,64},{48,80},{64,96},{80,112},{96,0},{112,16},{1... | collective-permute-start | bytes 393224 | tf_op jit(solution)/shard_map/ppermute | solution.py:428
  128.1 8.2 %collective-permute-start.20 = (bf16[512,128]{1,0:T(8,128)(2,1)S(1)}, bf16[512,128]{1,0:T(8,128)(2,1)S(1)}, u32[]{:S(2)}, u32[]{:S(2)}) collective-permute-start(bf16[512,128]{1,0:T(8,128)(2,1)S(1)} %get-tuple-element.30), channel_id=1, source_target_pairs={{0,64},{16,80},{32,96},{48,112},{64,0},{80,16},{96,32},{112,48},{1... | collective-permute-start | bytes 393224 | tf_op jit(solution)/shard_map/ppermute | solution.py:428
  131.7 5.5 %collective-permute-start.21 = (bf16[512,128]{1,0:T(8,128)(2,1)S(1)}, bf16[512,128]{1,0:T(8,128)(2,1)S(1)}, u32[]{:S(2)}, u32[]{:S(2)}) collective-permute-start(bf16[512,128]{1,0:T(8,128)(2,1)S(1)} %get-tuple-element.30), channel_id=1, source_target_pairs={{0,96},{16,112},{32,0},{48,16},{64,32},{80,48},{96,64},{112,80},{1... | collective-permute-start | bytes 393224 | tf_op jit(solution)/shard_map/ppermute | solution.py:428
  131.8 9.4 %collective-permute-start.15 = (bf16[512,128]{1,0:T(8,128)(2,1)S(1)}, bf16[512,128]{1,0:T(8,128)(2,1)S(1)}, u32[]{:S(2)}, u32[]{:S(2)}) collective-permute-start(bf16[512,128]{1,0:T(8,128)(2,1)S(1)} %get-tuple-element.31), channel_id=1, source_target_pairs={{0,32},{16,48},{32,64},{48,80},{64,96},{80,112},{96,0},{112,16},{1... | collective-permute-start | bytes 393224 | tf_op jit(solution)/shard_map/ppermute | solution.py:428
  133.2 8.8 %collective-permute-start.16 = (bf16[512,128]{1,0:T(8,128)(2,1)S(1)}, bf16[512,128]{1,0:T(8,128)(2,1)S(1)}, u32[]{:S(2)}, u32[]{:S(2)}) collective-permute-start(bf16[512,128]{1,0:T(8,128)(2,1)S(1)} %get-tuple-element.31), channel_id=1, source_target_pairs={{0,64},{16,80},{32,96},{48,112},{64,0},{80,16},{96,32},{112,48},{1... | collective-permute-start | bytes 393224 | tf_op jit(solution)/shard_map/ppermute | solution.py:428
  133.2 9.7 %collective-permute-start.17 = (bf16[512,128]{1,0:T(8,128)(2,1)S(1)}, bf16[512,128]{1,0:T(8,128)(2,1)S(1)}, u32[]{:S(2)}, u32[]{:S(2)}) collective-permute-start(bf16[512,128]{1,0:T(8,128)(2,1)S(1)} %get-tuple-element.31), channel_id=1, source_target_pairs={{0,96},{16,112},{32,0},{48,16},{64,32},{80,48},{96,64},{112,80},{1... | collective-permute-start | bytes 393224 | tf_op jit(solution)/shard_map/ppermute | solution.py:428
  137.3 7.5 %collective-permute-start.22 = (bf16[4,512,128]{2,1,0:T(8,128)(2,1)S(1)}, bf16[4,512,128]{2,1,0:T(8,128)(2,1)}, u32[]{:S(2)}, u32[]{:S(2)}) collective-permute-start(bf16[4,512,128]{2,1,0:T(8,128)(2,1)S(1)} %pad_maximum_fusion.1.here), channel_id=1, source_target_pairs={{0,16},{16,0},{32,48},{48,32},{64,80},{80,64},{96,112},{112,96},{1... | collective-permute-start | bytes 1572872 | tf_op jit(solution)/shard_map/ppermute | solution.py:432
  142.9 7.3 %collective-permute-start.18 = (bf16[4,512,128]{2,1,0:T(8,128)(2,1)S(1)}, bf16[4,512,128]{2,1,0:T(8,128)(2,1)}, u32[]{:S(2)}, u32[]{:S(2)}) collective-permute-start(bf16[4,512,128]{2,1,0:T(8,128)(2,1)S(1)} %pad_maximum_fusion.here), channel_id=1, source_target_pairs={{0,16},{16,0},{32,48},{48,32},{64,80},{80,64},{96,112},{112,96},{1... | collective-permute-start | bytes 1572872 | tf_op jit(solution)/shard_map/ppermute | solution.py:432
  (15 other events, 67.2 us)
